TPU v7x, 32 devices: a whole 2x2x4 slice. The times are simulated.
32 devices in a mesh: dp: 8 (over y, x, core), eshard: 4 (over z).
Axes of the slice: x: 2, y: 2, z: 4, core: 2. Of those that a mesh axis runs over, the one named last changes fastest.
Arguments:
- tokens: bfloat16 [2048, 4096], P('dp', 'eshard'), may hold values from -6 to 6
- cotangent: bfloat16 [2048, 4096], P('dp', 'eshard'), may hold values from -6 to 6
- route_ids: int32 [2048, 2], P('dp'), may hold values from 0 to 63, all different within a row; in each aligned block of 256 rows (0 to 255, 256 to 511, ...) at most 16 rows name the same one
- gate_fixed: int32 [2048, 2], P('dp'), may hold values from 1 to 65535
- w_gate: bfloat16 [4096, 32768], P('eshard', 'dp'), may hold values from -0.09375 to 0.09375
- w_up: bfloat16 [4096, 32768], P('eshard', 'dp'), may hold values from -0.09375 to 0.09375
- w_down: bfloat16 [32768, 4096], P('dp', 'eshard'), may hold values from -0.0625 to 0.0625
Outputs:
- mixed: bfloat16 [2048, 4096], P('dp', 'eshard')
- token_grad: bfloat16 [2048, 4096], P('dp', 'eshard')
- grad_w_gate: bfloat16 [4096, 32768], P('eshard', 'dp')
- grad_w_up: bfloat16 [4096, 32768], P('eshard', 'dp')
- grad_w_down: bfloat16 [32768, 4096], P('dp', 'eshard')
Inputs may be any that keep to these rules, and one draw needn't show every extreme that they name: `route_ids`: the two ids of a token differ; among the 256 tokens of one index of dp, no id is named by more than 16 routes, a bound that some block reaches.
All inputs are finite; a program needn't handle non-finite values.
Results may differ from a plain program's by a relative error of at most 0.028.
Values may be sent and summed in bfloat16 or wider, within the bound.
A program may use at most 128 MiB of HBM per device.

v0:
```python
import jax
import jax.numpy as jnp
from jax import lax
from jax.sharding import PartitionSpec as P

EXPERTS = 4
CAP = 16


def for_sending(shard):

    def short(part):
        return part.astype(jnp.bfloat16) if part.dtype == jnp.float32 else part

    return jax.tree.map(short, shard)


def routing(ids, gates):
    expert_ids = jnp.arange(EXPERTS, dtype=jnp.int32)
    hits = (ids[:, :, None] == expert_ids[None, None, :]).astype(jnp.int32)
    hit_tok = jnp.sum(hits, axis=1)
    gate_values = gates.astype(jnp.float32) / 65536.0
    weight_tok = jnp.sum(hits.astype(jnp.float32) * gate_values[:, :, None], axis=1)
    slots = jnp.cumsum(hit_tok, axis=0) - hit_tok
    target = expert_ids[None, :] * CAP + slots
    rows = jnp.arange(EXPERTS * CAP, dtype=jnp.int32)
    match = (target[None, :, :] == rows[:, None, None]).astype(jnp.float32) * hit_tok[
        None, :, :
    ].astype(jnp.float32)
    select = jnp.sum(match, axis=2)
    weighted = jnp.sum(match * weight_tok[None, :, :], axis=2)
    return (select, weighted)


def activate(gate_pre, up_pre):
    return (gate_pre * jax.nn.sigmoid(gate_pre) * up_pre).astype(jnp.bfloat16)


def derivative(grad_hidden, gate_pre, up_pre):
    logistic = jax.nn.sigmoid(gate_pre)
    gate_grad = grad_hidden * up_pre * logistic * (1.0 + gate_pre * (1.0 - logistic))
    up_grad = grad_hidden * gate_pre * logistic
    return (gate_grad.astype(jnp.bfloat16), up_grad.astype(jnp.bfloat16))


def contract_rows(left, right):
    return lax.dot_general(
        left, right, (((0,), (0,)), ((), ())), preferred_element_type=jnp.float32
    )


def contract_cols(left, right):
    return lax.dot_general(
        left, right, (((1,), (1,)), ((), ())), preferred_element_type=jnp.float32
    )


def on_device(tokens, cotangent, route_ids, gate_fixed, w_gate, w_up, w_down):
    groups = lax.axis_size("dp")
    members = groups // EXPERTS
    features = tokens.shape[1]
    highest = lax.Precision.HIGHEST
    select, weighted = routing(route_ids, gate_fixed)
    capacity = select.shape[0] // EXPERTS
    token_rows = jnp.dot(
        select.astype(jnp.bfloat16), tokens, preferred_element_type=jnp.float32
    ).astype(jnp.bfloat16)
    scaled_rows = jnp.dot(weighted, cotangent.astype(jnp.float32), precision=highest).astype(
        jnp.bfloat16
    )
    send_tokens = jnp.repeat(token_rows.reshape(EXPERTS, capacity, features), members, axis=0)
    send_grads = jnp.repeat(scaled_rows.reshape(EXPERTS, capacity, features), members, axis=0)
    recv_tokens, recv_grads = (
        lax.all_to_all(send_tokens, "dp", split_axis=0, concat_axis=0, tiled=True),
        lax.all_to_all(send_grads, "dp", split_axis=0, concat_axis=0, tiled=True),
    )
    inputs = recv_tokens.reshape(groups * capacity, features)
    route_grad = recv_grads.reshape(groups * capacity, features)
    gate_part = jnp.dot(inputs, w_gate, preferred_element_type=jnp.float32)
    up_part = jnp.dot(inputs, w_up, preferred_element_type=jnp.float32)
    gate_pre, up_pre = (
        lax.psum_scatter(
            gate_part.astype(jnp.bfloat16), "eshard", scatter_dimension=0, tiled=True
        ).astype(jnp.float32),
        lax.psum_scatter(
            up_part.astype(jnp.bfloat16), "eshard", scatter_dimension=0, tiled=True
        ).astype(jnp.float32),
    )
    hidden = lax.all_gather(activate(gate_pre, up_pre), "eshard", axis=0, tiled=True)
    out_part = jnp.dot(hidden, w_down, preferred_element_type=jnp.float32).reshape(
        groups, capacity, features
    )
    hidden_part = contract_cols(route_grad, w_down)
    grad_hidden = lax.psum_scatter(
        hidden_part.astype(jnp.bfloat16), "eshard", scatter_dimension=0, tiled=True
    ).astype(jnp.float32)
    gate_grad, up_grad = lax.all_gather(
        for_sending(derivative(grad_hidden, gate_pre, up_pre)), "eshard", axis=0, tiled=True
    )
    grad_w_gate = contract_rows(inputs, gate_grad).astype(jnp.bfloat16)
    grad_w_up = contract_rows(inputs, up_grad).astype(jnp.bfloat16)
    grad_w_down = contract_rows(hidden, route_grad).astype(jnp.bfloat16)
    back_part = contract_cols(gate_grad, w_gate) + contract_cols(up_grad, w_up)
    back_part = back_part.reshape(groups, capacity, features)
    out_back, back_back = (
        lax.all_to_all(
            out_part.astype(jnp.bfloat16), "dp", split_axis=0, concat_axis=0, tiled=True
        ).astype(out_part.dtype),
        lax.all_to_all(
            back_part.astype(jnp.bfloat16), "dp", split_axis=0, concat_axis=0, tiled=True
        ).astype(back_part.dtype),
    )
    out_rows = jnp.sum(out_back.reshape(EXPERTS, members, capacity, features), axis=1).reshape(
        EXPERTS * capacity, features
    )
    back_rows = jnp.sum(back_back.reshape(EXPERTS, members, capacity, features), axis=1).reshape(
        EXPERTS * capacity, features
    )
    mixed = jnp.dot(jnp.transpose(weighted), out_rows, precision=highest).astype(jnp.bfloat16)
    token_grad = jnp.dot(jnp.transpose(select), back_rows, precision=highest).astype(jnp.bfloat16)
    return (mixed, token_grad, grad_w_gate, grad_w_up, grad_w_down)


def solution(mesh):
    placed = (
        P("dp", "eshard"),
        P("dp", "eshard"),
        P("dp", None),
        P("dp", None),
        P("eshard", "dp"),
        P("eshard", "dp"),
        P("dp", "eshard"),
    )
    return jax.shard_map(
        on_device,
        mesh=mesh,
        in_specs=placed,
        out_specs=(
            P("dp", "eshard"),
            P("dp", "eshard"),
            P("eshard", "dp"),
            P("eshard", "dp"),
            P("dp", "eshard"),
        ),
        check_vma=False,
    )
```

profile of v0, /device:TPU:0, one launch (start us, length us, event | category | flops | bytes accessed | tf_op | source)
XLA Modules:
  0.0 231.6 jit_solution(17192119187392792995)
XLA Ops:
  7.2 0.0 copy-start
  7.2 0.0 reduce-scatter.4.cloned.1.call-start
  7.2 0.7 convert_reduce_fusion.2
  8.0 1.2 reduce-window.6
  9.2 0.1 slice.8
  9.3 0.1 copy.18
  9.4 0.1 copy.19
  9.5 0.1 add_bitcast_fusion
  9.6 0.7 convert_multiply_fusion.5
  10.3 0.7 fusion.14
  11.0 0.1 fusion.16
  11.1 0.2 convolution_convert_fusion.10
  11.4 11.9 %all_to_all.20 = bf16[8,16,1024]{2,1,0:T(8,128)(2,1)S(1)} all-to-all(bf16[8,16,1024]{2,1,0:T(8,128)(2,1)S(1)} %bitcast.65), channel_id=1, replica_groups=mesh['dp'=8,'eshard'=4] {'dp'}, dimensions={0} | all-to-all | bytes 524288 | tf_op jit(solution)/shard_map/all_to_all | solution.py:74
  23.3 5.6 %convolution_convert_fusion.5 = bf16[128,4096]{1,0:T(8,128)(2,1)} fusion(bf16[128,1024]{1,0:T(8,128)(2,1)S(1)} %bitcast.57, bf16[1024,4096]{1,0:T(8,128)(2,1)} %param.11), kind=kOutput, calls=%fused_computation.5 | convolution fusion | flops 1074266112 | bytes 9699328 | tf_op jit(solution)/shard_map/dot_general | solution.py:79
  28.9 0.0 reduce-scatter.4.cloned.1.call-update
  28.9 0.0 reduce-scatter.6.cloned.1.call-start
  29.0 5.7 %convolution_convert_fusion.4 = bf16[128,4096]{1,0:T(8,128)(2,1)} fusion(bf16[128,1024]{1,0:T(8,128)(2,1)S(1)} %bitcast.58, bf16[1024,4096]{1,0:T(8,128)(2,1)} %param.12), kind=kOutput, calls=%fused_computation.4 | convolution fusion | flops 1074266112 | bytes 9699328 | tf_op jit(solution)/shard_map/dot_general | solution.py:80
  34.6 0.0 reduce-scatter.6.cloned.1.call-update
  34.6 0.0 reduce-scatter.8.cloned.1.call-start
  34.7 0.4 convolution_convert_fusion.9
  35.1 9.3 %all_to_all.21 = bf16[8,16,1024]{2,1,0:T(8,128)(2,1)S(1)} all-to-all(bf16[8,16,1024]{2,1,0:T(8,128)(2,1)S(1)} %bitcast.66), channel_id=1, replica_groups=mesh['dp'=8,'eshard'=4] {'dp'}, dimensions={0} | all-to-all | bytes 524288 | tf_op jit(solution)/shard_map/all_to_all | solution.py:75
  44.4 7.3 %convolution_convert_fusion.3 = bf16[128,4096]{1,0:T(8,128)(2,1)} fusion(bf16[128,1024]{1,0:T(8,128)(2,1)S(1)} %bitcast.61, bf16[4096,1024]{1,0:T(8,128)(2,1)} %param.13), kind=kOutput, calls=%fused_computation.3 | convolution fusion | flops 1074266112 | bytes 9699328 | tf_op jit(solution)/shard_map/dot_general | solution.py:53
  51.7 0.0 reduce-scatter.8.cloned.1.call-update
  51.8 0.0 all-gather.6.cloned.1.call-start
  51.8 3.9 %reduce-scatter.4.cloned.1.call-done = bf16[32,4096]{1,0:T(8,128)(2,1)} async-done(((bf16[128,4096]{1,0:T(8,128)(2,1)}), bf16[32,4096]{1,0:T(8,128)(2,1)}) %reduce-scatter.4.cloned.1.call-update) | async-done | bytes 262160 | tf_op jit(solution)/shard_map/reduce_scatter | solution.py:82
  55.7 28.7 %reduce-scatter.6.cloned.1.call-done = bf16[32,4096]{1,0:T(8,128)(2,1)} async-done(((bf16[128,4096]{1,0:T(8,128)(2,1)}), bf16[32,4096]{1,0:T(8,128)(2,1)}) %reduce-scatter.6.cloned.1.call-update) | async-done | bytes 262160 | tf_op jit(solution)/shard_map/reduce_scatter | solution.py:85
  84.4 28.7 %reduce-scatter.8.cloned.1.call-done = bf16[32,4096]{1,0:T(8,128)(2,1)} async-done(((bf16[128,4096]{1,0:T(8,128)(2,1)}), bf16[32,4096]{1,0:T(8,128)(2,1)}) %reduce-scatter.8.cloned.1.call-update) | async-done | bytes 262160 | tf_op jit(solution)/shard_map/reduce_scatter | solution.py:94
  113.1 2.3 fusion.10
  115.4 0.0 all-gather.6.cloned.1.call-update
  115.4 0.0 all-gather.8.cloned.1.call-start
  115.4 0.5 all-gather.8.cloned.1.call-update
  116.0 0.0 all-gather.4.cloned.1.call-start
  116.0 0.5 all-gather.4.cloned.1.call-update
  116.5 25.5 %all-gather.6.cloned.1.call-done = bf16[128,4096]{1,0:T(8,128)(2,1)} async-done(((bf16[32,4096]{1,0:T(8,128)(2,1)}), bf16[128,4096]{1,0:T(8,128)(2,1)}) %all-gather.6.cloned.1.call-update) | async-done | bytes 1048592 | tf_op jit(solution)/shard_map/all_gather | solution.py:97
  142.0 6.6 %fusion.17 = f32[128,1024]{1,0:T(8,128)S(1)} fusion(bf16[128,4096]{1,0:T(8,128)(2,1)} %all-gather.6.cloned.1.call-done, bf16[1024,4096]{1,0:T(8,128)(2,1)} %param.11), kind=kOutput, calls=%fused_computation.47 | convolution fusion | flops 1073741824 | bytes 9961472 | tf_op jit(solution)/shard_map/dot_general | solution.py:53
  148.7 22.8 %all-gather.8.cloned.1.call-done = bf16[128,4096]{1,0:T(8,128)(2,1)} async-done(((bf16[32,4096]{1,0:T(8,128)(2,1)}), bf16[128,4096]{1,0:T(8,128)(2,1)}) %all-gather.8.cloned.1.call-update) | async-done | bytes 1048592 | tf_op jit(solution)/shard_map/all_gather | solution.py:97
  171.4 7.4 %fusion = bf16[128,1024]{1,0:T(8,128)(2,1)} fusion(f32[128,1024]{1,0:T(8,128)S(1)} %fusion.17, bf16[128,4096]{1,0:T(8,128)(2,1)} %all-gather.8.cloned.1.call-done, bf16[1024,4096]{1,0:T(8,128)(2,1)} %param.12), kind=kOutput, calls=%fused_computation.9 | convolution fusion | flops 1074003968 | bytes 10223616 | tf_op jit(solution)/shard_map/dot_general | solution.py:53
  178.8 3.8 %all-to-all-start.3 = ((bf16[8,16,1024]{2,1,0:T(8,128)(2,1)}), bf16[8,16,1024]{2,1,0:T(8,128)(2,1)S(1)}, u32[]{:S(2)}, u32[]{:S(2)}) async-start(bf16[8,16,1024]{2,1,0:T(8,128)(2,1)} %bitcast.12), calls=%async_computation.6 | async-start | bytes 524288 | tf_op jit(solution)/shard_map/all_to_all | solution.py:109
  182.6 5.8 %convolution_convert_fusion.1 = bf16[1024,4096]{1,0:T(8,128)(2,1)} fusion(bf16[128,1024]{1,0:T(8,128)(2,1)S(1)} %bitcast.59, bf16[128,4096]{1,0:T(8,128)(2,1)S(1)} %copy-done.3), kind=kOutput, calls=%fused_computation.1 | convolution fusion | flops 1077936128 | bytes 9699328 | tf_op jit(solution)/shard_map/dot_general | solution.py:47
  188.4 5.8 %convolution_convert_fusion.2 = bf16[1024,4096]{1,0:T(8,128)(2,1)} fusion(bf16[128,1024]{1,0:T(8,128)(2,1)S(1)} %bitcast.60, bf16[128,4096]{1,0:T(8,128)(2,1)S(1)} %copy-done.2), kind=kOutput, calls=%fused_computation.2 | convolution fusion | flops 1077936128 | bytes 9699328 | tf_op jit(solution)/shard_map/dot_general | solution.py:47
  194.2 6.7 %all-gather.4.cloned.1.call-done = bf16[128,4096]{1,0:T(8,128)(2,1)} async-done(((bf16[32,4096]{1,0:T(8,128)(2,1)}), bf16[128,4096]{1,0:T(8,128)(2,1)}) %all-gather.4.cloned.1.call-update) | async-done | bytes 1048592 | tf_op jit(solution)/shard_map/all_gather | solution.py:89
  200.8 5.7 %convolution_convert_fusion.8 = bf16[128,1024]{1,0:T(8,128)(2,1)} fusion(bf16[128,4096]{1,0:T(8,128)(2,1)} %all-gather.4.cloned.1.call-done, bf16[4096,1024]{1,0:T(8,128)(2,1)} %param.13), kind=kOutput, calls=%fused_computation.10 | convolution fusion | flops 1073872896 | bytes 9699328 | tf_op jit(solution)/shard_map/dot_general | solution.py:90
  206.6 5.8 %convolution_convert_fusion = bf16[4096,1024]{1,0:T(8,128)(2,1)} fusion(bf16[128,4096]{1,0:T(8,128)(2,1)S(1)} %copy-done.1, bf16[128,1024]{1,0:T(8,128)(2,1)S(1)} %bitcast.62), kind=kOutput, calls=%fused_computation | convolution fusion | flops 1077936128 | bytes 9699328 | tf_op jit(solution)/shard_map/dot_general | solution.py:47
  212.3 0.0 all-to-all-done.3
  212.3 3.7 %all-to-all-start.1 = ((bf16[8,16,1024]{2,1,0:T(8,128)(2,1)}), bf16[8,16,1024]{2,1,0:T(8,128)(2,1)S(1)}, u32[]{:S(2)}, u32[]{:S(2)}) async-start(bf16[8,16,1024]{2,1,0:T(8,128)(2,1)} %bitcast.6), calls=%async_computation.3 | async-start | bytes 524288 | tf_op jit(solution)/shard_map/all_to_all | solution.py:106
  216.0 1.8 convolution_convert_fusion.6
  217.9 5.0 %all-to-all-done.1 = bf16[8,16,1024]{2,1,0:T(8,128)(2,1)S(1)} async-done(((bf16[8,16,1024]{2,1,0:T(8,128)(2,1)}), bf16[8,16,1024]{2,1,0:T(8,128)(2,1)S(1)}, u32[]{:S(2)}, u32[]{:S(2)}) %all-to-all-start.1) | async-done | bytes 262176 | tf_op jit(solution)/shard_map/all_to_all | solution.py:106
  222.9 1.8 convolution_convert_fusion.7
  (18 shorter events, 0.2 us)
Async XLA Ops:
  7.2 3.9 %copy-start = (bf16[256,1024]{1,0:T(8,128)(2,1)S(1)}, bf16[256,1024]{1,0:T(8,128)(2,1)}, u32[]{:S(2)}) copy-start(bf16[256,1024]{1,0:T(8,128)(2,1)} %param.7) | copy-start | bytes 1572868
  7.2 48.5 %reduce-scatter.4.cloned.1.call-start = ((), (), s32[]{:S(2)}) async-start(), calls=%async_computation.7 | async-start | bytes 1310720 | tf_op jit(solution)/shard_map/reduce_scatter | solution.py:82
  28.9 5.8 %copy-start.4 = (bf16[256,1024]{1,0:T(8,128)(2,1)S(1)}, bf16[256,1024]{1,0:T(8,128)(2,1)}, u32[]{:S(2)}) copy-start(bf16[256,1024]{1,0:T(8,128)(2,1)} %param.8) | copy-start | bytes 1572868
  28.9 55.5 %reduce-scatter.6.cloned.1.call-start = ((), (), s32[]{:S(2)}) async-start(), calls=%async_computation.8 | async-start | bytes 1310720 | tf_op jit(solution)/shard_map/reduce_scatter | solution.py:85
  34.6 78.4 %reduce-scatter.8.cloned.1.call-start = ((), (), s32[]{:S(2)}) async-start(), calls=%async_computation.10 | async-start | bytes 1310720 | tf_op jit(solution)/shard_map/reduce_scatter | solution.py:94
  51.8 90.3 %all-gather.6.cloned.1.call-start = ((), (), s32[]{:S(2)}) async-start(), calls=%async_computation.11 | async-start | bytes 1310720 | tf_op jit(solution)/shard_map/all_gather | solution.py:97
  115.4 56.0 %all-gather.8.cloned.1.call-start = ((), (), s32[]{:S(2)}) async-start(), calls=%async_computation.12 | async-start | bytes 1310720 | tf_op jit(solution)/shard_map/all_gather | solution.py:97
  116.0 84.8 %all-gather.4.cloned.1.call-start = ((), (), s32[]{:S(2)}) async-start(), calls=%async_computation.9 | async-start | bytes 1310720 | tf_op jit(solution)/shard_map/all_gather | solution.py:89
  171.4 11.2 %copy-start.3 = (bf16[128,4096]{1,0:T(8,128)(2,1)S(1)}, bf16[128,4096]{1,0:T(8,128)(2,1)}, u32[]{:S(2)}) copy-start(bf16[128,4096]{1,0:T(8,128)(2,1)} %all-gather.8.cloned.1.call-done) | copy-start | bytes 3145732
  178.8 9.6 %copy-start.2 = (bf16[128,4096]{1,0:T(8,128)(2,1)S(1)}, bf16[128,4096]{1,0:T(8,128)(2,1)}, u32[]{:S(2)}) copy-start(bf16[128,4096]{1,0:T(8,128)(2,1)} %all-gather.6.cloned.1.call-done) | copy-start | bytes 3145732
  178.8 33.5 %all-to-all-start.3 = ((bf16[8,16,1024]{2,1,0:T(8,128)(2,1)}), bf16[8,16,1024]{2,1,0:T(8,128)(2,1)S(1)}, u32[]{:S(2)}, u32[]{:S(2)}) async-start(bf16[8,16,1024]{2,1,0:T(8,128)(2,1)} %bitcast.12), calls=%async_computation.6 | async-start | bytes 524288 | tf_op jit(solution)/shard_map/all_to_all | solution.py:109
  200.8 5.7 %copy-start.1 = (bf16[128,4096]{1,0:T(8,128)(2,1)S(1)}, bf16[128,4096]{1,0:T(8,128)(2,1)}, u32[]{:S(2)}) copy-start(bf16[128,4096]{1,0:T(8,128)(2,1)} %all-gather.4.cloned.1.call-done) | copy-start | bytes 3145732
  212.3 10.6 %all-to-all-start.1 = ((bf16[8,16,1024]{2,1,0:T(8,128)(2,1)}), bf16[8,16,1024]{2,1,0:T(8,128)(2,1)S(1)}, u32[]{:S(2)}, u32[]{:S(2)}) async-start(bf16[8,16,1024]{2,1,0:T(8,128)(2,1)} %bitcast.6), calls=%async_computation.3 | async-start | bytes 524288 | tf_op jit(solution)/shard_map/all_to_all | solution.py:106
Sparse Core Ops, SparseCore 0:
  29.0 26.6 reduce-scatter.3
  58.6 25.7 reduce-scatter.5
  87.3 25.7 reduce-scatter.7
  115.5 26.4 all-gather.5
  144.0 27.3 all-gather.7
  173.4 27.3 all-gather.3
where the time goes:
time: 232 us
  waiting for transfers between devices  122 us (53%)
  matrix products  59.9 us (26%)
  blocking collectives  21.2 us (9%)
  between operations  14.2 us (6%)
  starting transfers between devices  7.69 us (3%)
  other arithmetic  5.91 us (3%)
    all_gather x2, waiting for transfers between devices, on_device(): lax.all_gather(for_sending(derivative(grad_hidden, gate_pre, up_pre)), 'e...  48.3 us
    reduce_scatter x1, waiting for transfers between devices, on_device(): lax.psum_scatter(up_part.astype(jnp.bfloat16), 'eshard', scatter_dimensio...  28.7 us
    reduce_scatter x1, waiting for transfers between devices, on_device(): lax.psum_scatter(hidden_part.astype(jnp.bfloat16), 'eshard', scatter_dime...  28.7 us
    dot_general x3, matrix products, contract_cols(): lax.dot_general(left, right, (((1,), (1,)), ((), ())), preferred_element_...  21.3 us
    dot_general x3, matrix products, contract_rows(): lax.dot_general(left, right, (((0,), (0,)), ((), ())), preferred_element_...  17.3 us
    all_to_all x1, blocking collectives, on_device(): lax.all_to_all(send_tokens, 'dp', split_axis=0, concat_axis=0, tiled=True)  11.9 us
    all_to_all x1, blocking collectives, on_device(): lax.all_to_all(send_grads, 'dp', split_axis=0, concat_axis=0, tiled=True)  9.32 us
    all_gather x1, waiting for transfers between devices, on_device(): lax.all_gather(activate(gate_pre, up_pre), 'eshard', axis=0, tiled=True)  6.65 us
  transfers between devices with their start and end apart: 8, of which 7 were waited for; matrix products, arithmetic and copies ran while one was open for 23% of the time, Pallas kernels for 0%

commit v1 on v0

v1 whole, which is shorter than its diff:
```python
import functools

import jax
import jax.numpy as jnp
from jax import lax
from jax.experimental import pallas as pl
from jax.experimental.pallas import tpu as pltpu
from jax.sharding import PartitionSpec as P

EXPERTS = 4
CAP = 16
WIDTH = 256
VMEM_BYTES = 60 * 1024 * 1024


def routing(ids, gates):
    expert_ids = jnp.arange(EXPERTS, dtype=jnp.int32)
    hits = (ids[:, :, None] == expert_ids[None, None, :]).astype(jnp.int32)
    hit_tok = jnp.sum(hits, axis=1)
    gate_values = gates.astype(jnp.float32) / 65536.0
    weight_tok = jnp.sum(hits.astype(jnp.float32) * gate_values[:, :, None], axis=1)
    slots = jnp.cumsum(hit_tok, axis=0) - hit_tok
    target = expert_ids[None, :] * CAP + slots
    rows = jnp.arange(EXPERTS * CAP, dtype=jnp.int32)
    match = (target[None, :, :] == rows[:, None, None]).astype(jnp.float32) * hit_tok[
        None, :, :
    ].astype(jnp.float32)
    select = jnp.sum(match, axis=2)
    weighted = jnp.sum(match * weight_tok[None, :, :], axis=2)
    return (select, weighted)


MESH = pl.DeviceIdType.MESH


def contract_cols(left, right):
    return lax.dot_general(
        left, right, (((1,), (1,)), ((), ())), preferred_element_type=jnp.float32
    )


def contract_rows(left, right):
    return lax.dot_general(
        left, right, (((0,), (0,)), ((), ())), preferred_element_type=jnp.float32
    )


def window_kernel(
    size, groups, members, chunks, width,
    tok_ref, grd_ref, wg_ref, wu_ref, wd_ref,
    hid_ref, gg_ref, ug_ref, x_ref, g_ref, back_ref,
    wg_v, wu_v, wd_v, x_v, g_v, part, outer, inner, full, out_acc, back_acc, y_send, y_recv,
    w_sem, xs_sem, xr_sem, in_sem, outer_sem, inner_sem, out_sem, ys_sem, yr_sem,
):
    me, z = lax.axis_index("dp"), lax.axis_index("eshard")
    cap = tok_ref.shape[0] // EXPERTS
    feats = tok_ref.shape[1]
    rows = groups * cap
    half = size // 2
    left = z < half
    middle = jnp.logical_or(z == half - 1, z == half)
    tip = jnp.logical_or(z == 0, z == size - 1)
    inward = jnp.where(left, z + 1, z - 1)
    outward = jnp.where(tip, z, jnp.where(left, z - 1, z + 1))
    distance = jnp.where(left, half - 1 - z, z - half)

    def weight_copies(c):
        cols = pl.ds(pl.multiple_of(c * width, width), width)
        return (
            pltpu.make_async_copy(wg_ref.at[:, cols], wg_v.at[c], w_sem.at[c, 0]),
            pltpu.make_async_copy(wu_ref.at[:, cols], wu_v.at[c], w_sem.at[c, 1]),
            pltpu.make_async_copy(wd_ref.at[cols, :], wd_v.at[c], w_sem.at[c, 2]),
        )

    @pl.loop(0, chunks)
    def _(c):
        for copy in weight_copies(c):
            copy.start()

    barrier = pltpu.get_barrier_semaphore()

    @pl.loop(1, groups)
    def _(k):
        pl.semaphore_signal(
            barrier, inc=1, device_id={"dp": lax.rem(me + k, groups)}, device_id_type=MESH
        )

    pl.semaphore_signal(barrier, inc=1, device_id={"eshard": inward}, device_id_type=MESH)

    @pl.when(jnp.logical_not(tip))
    def _():
        pl.semaphore_signal(barrier, inc=1, device_id={"eshard": outward}, device_id_type=MESH)

    pl.semaphore_wait(barrier, groups + jnp.where(tip, 0, 1))

    def row_copy(src, dst, which, k):
        to = lax.rem(me + k, groups)
        first = pl.multiple_of((to // members) * cap, cap)
        return pltpu.make_async_remote_copy(
            src_ref=src.at[pl.ds(first, cap), :],
            dst_ref=dst.at[me],
            send_sem=xs_sem.at[which, k],
            recv_sem=xr_sem.at[which, k],
            device_id={"dp": to},
            device_id_type=MESH,
        )

    for which, (src, dst) in enumerate(((tok_ref, x_v), (grd_ref, g_v))):

        @pl.loop(1, groups)
        def _(k):
            row_copy(src, dst, which, k).start()

        own = pl.multiple_of((me // members) * cap, cap)
        dst[me] = src[pl.ds(own, cap), :]

    for which, (src, dst) in enumerate(((tok_ref, x_v), (grd_ref, g_v))):

        @pl.loop(1, groups)
        def _(k):
            row_copy(src, dst, which, k).wait()

    x_ref[...] = x_v[...].reshape(rows, feats)
    g_ref[...] = g_v[...].reshape(rows, feats)
    out_acc[...] = jnp.zeros_like(out_acc)
    back_acc[...] = jnp.zeros_like(back_acc)

    def to_outer(c, k):
        return pltpu.make_async_remote_copy(
            src_ref=part.at[c, k], dst_ref=outer.at[c, k],
            send_sem=in_sem.at[c, k], recv_sem=outer_sem.at[c, k],
            device_id={"eshard": inward}, device_id_type=MESH,
        )

    def to_partner(c, k):
        return pltpu.make_async_remote_copy(
            src_ref=part.at[c, k], dst_ref=inner.at[c, k],
            send_sem=in_sem.at[c, k], recv_sem=inner_sem.at[c, k],
            device_id={"eshard": inward}, device_id_type=MESH,
        )

    def sum_out(c, k):
        return pltpu.make_async_remote_copy(
            src_ref=full.at[c, k], dst_ref=inner.at[c, k],
            send_sem=out_sem.at[c, k], recv_sem=inner_sem.at[c, k],
            device_id={"eshard": outward}, device_id_type=MESH,
        )

    def pass_out(c, k):
        return pltpu.make_async_remote_copy(
            src_ref=inner.at[c, k], dst_ref=inner.at[c, k],
            send_sem=out_sem.at[c, k], recv_sem=inner_sem.at[c, k],
            device_id={"eshard": outward}, device_id_type=MESH,
        )

    def gather_in(c):
        for copy in weight_copies(c):
            copy.wait()
        for k in range(3):
            if k == 0:
                own = jnp.dot(x_ref[...], wg_v[c], preferred_element_type=jnp.float32)
            elif k == 1:
                own = jnp.dot(x_ref[...], wu_v[c], preferred_element_type=jnp.float32)
            else:
                own = contract_cols(g_ref[...], wd_v[c])

            @pl.when(tip)
            def _():
                part[c, k] = own.astype(jnp.bfloat16)

            @pl.when(jnp.logical_not(tip))
            def _():
                to_outer(c, k).wait_recv()
                part[c, k] = (own + outer[c, k].astype(jnp.float32)).astype(jnp.bfloat16)

            @pl.when(middle)
            def _():
                to_partner(c, k).start()

            @pl.when(jnp.logical_not(middle))
            def _():
                to_outer(c, k).start()

    def finish(c):
        for k in range(3):
            to_partner(c, k).wait_recv()

            @pl.when(middle)
            def _():
                full[c, k] = (
                    part[c, k].astype(jnp.float32) + inner[c, k].astype(jnp.float32)
                ).astype(jnp.bfloat16)

            @pl.when(jnp.logical_and(middle, jnp.logical_not(tip)))
            def _():
                sum_out(c, k).start()

            @pl.when(jnp.logical_not(jnp.logical_or(middle, tip)))
            def _():
                pass_out(c, k).start()

        def summed(k):
            mine = part[c, k].astype(jnp.float32)
            return inner[c, k].astype(jnp.float32) + jnp.where(middle, mine, jnp.zeros_like(mine))

        gate, up, down = summed(0), summed(1), summed(2)
        logistic = 1.0 / (1.0 + jnp.exp(-gate))
        silu = gate * logistic
        hidden = (silu * up).astype(jnp.bfloat16)
        gate_grad = (down * up * logistic * (1.0 + gate * (1.0 - logistic))).astype(jnp.bfloat16)
        up_grad = (down * silu).astype(jnp.bfloat16)
        cols = pl.ds(pl.multiple_of(c * width, width), width)
        hid_ref[:, cols] = hidden
        gg_ref[:, cols] = gate_grad
        ug_ref[:, cols] = up_grad
        out_acc[...] += jnp.dot(hidden, wd_v[c], preferred_element_type=jnp.float32)
        back_acc[...] += contract_cols(gate_grad, wg_v[c]) + contract_cols(up_grad, wu_v[c])

    lag = jnp.where(middle, 1, 1 + 4 * distance)

    @pl.loop(0, chunks + 1 + 4 * (half - 1))
    def _(t):
        @pl.when(t < chunks)
        def _():
            gather_in(t)

        @pl.when(jnp.logical_and(t >= lag, t - lag < chunks))
        def _():
            finish(t - lag)

    y_send[0] = out_acc[...].astype(jnp.bfloat16).reshape(groups, cap, feats)
    y_send[1] = back_acc[...].astype(jnp.bfloat16).reshape(groups, cap, feats)

    def return_copy(which, k):
        to = lax.rem(me + k, groups)
        return pltpu.make_async_remote_copy(
            src_ref=y_send.at[which, to], dst_ref=y_recv.at[which, me],
            send_sem=ys_sem.at[which, k], recv_sem=yr_sem.at[which, k],
            device_id={"dp": to}, device_id_type=MESH,
        )

    for which in range(2):

        @pl.loop(1, groups)
        def _(k):
            return_copy(which, k).start()

        y_recv[which, me] = y_send[which, me]

    @pl.loop(0, chunks)
    def _(c):
        for k in range(3):
            to_outer(c, k).wait_send()

            @pl.when(jnp.logical_not(tip))
            def _():
                sum_out(c, k).wait_send()

    for which in range(2):

        @pl.loop(1, groups)
        def _(k):
            return_copy(which, k).wait()

    back_ref[...] = y_recv[...]


def run_window(token_rows, scaled_rows, w_gate, w_up, w_down):
    groups, size = lax.axis_size("dp"), lax.axis_size("eshard")
    members = groups // EXPERTS
    feats, hidden = w_gate.shape
    cap = token_rows.shape[0] // EXPERTS
    rows = groups * cap
    width = min(WIDTH, hidden)
    chunks = hidden // width
    bf16, f32 = jnp.bfloat16, jnp.float32
    vmem, hbm = pl.BlockSpec(memory_space=pltpu.VMEM), pl.BlockSpec(memory_space=pl.ANY)
    dma = pltpu.SemaphoreType.DMA
    wide = jax.ShapeDtypeStruct((rows, hidden), bf16)
    deep = jax.ShapeDtypeStruct((rows, feats), bf16)
    stage = pltpu.VMEM((chunks, 3, rows, width), bf16)
    return pl.pallas_call(
        functools.partial(window_kernel, size, groups, members, chunks, width),
        out_shape=(
            wide, wide, wide, deep, deep,
            jax.ShapeDtypeStruct((2, groups, cap, feats), bf16),
        ),
        in_specs=[vmem, vmem, hbm, hbm, hbm],
        out_specs=(vmem,) * 6,
        scratch_shapes=[
            pltpu.VMEM((chunks, feats, width), bf16),
            pltpu.VMEM((chunks, feats, width), bf16),
            pltpu.VMEM((chunks, width, feats), bf16),
            pltpu.VMEM((groups, cap, feats), bf16),
            pltpu.VMEM((groups, cap, feats), bf16),
            stage, stage, stage, stage,
            pltpu.VMEM((rows, feats), f32),
            pltpu.VMEM((rows, feats), f32),
            pltpu.VMEM((2, groups, cap, feats), bf16),
            pltpu.VMEM((2, groups, cap, feats), bf16),
            dma((chunks, 3)),
            dma((2, groups)), dma((2, groups)),
            dma((chunks, 3)), dma((chunks, 3)), dma((chunks, 3)), dma((chunks, 3)),
            dma((2, groups)), dma((2, groups)),
        ],
        compiler_params=pltpu.CompilerParams(
            collective_id=0, has_side_effects=True, vmem_limit_bytes=VMEM_BYTES
        ),
    )(token_rows, scaled_rows, w_gate, w_up, w_down)


def on_device(tokens, cotangent, route_ids, gate_fixed, w_gate, w_up, w_down):
    groups = lax.axis_size("dp")
    members = groups // EXPERTS
    features = tokens.shape[1]
    highest = lax.Precision.HIGHEST
    select, weighted = routing(route_ids, gate_fixed)
    capacity = select.shape[0] // EXPERTS
    token_rows = jnp.dot(
        select.astype(jnp.bfloat16), tokens, preferred_element_type=jnp.float32
    ).astype(jnp.bfloat16)
    scaled_rows = jnp.dot(weighted, cotangent.astype(jnp.float32), precision=highest).astype(
        jnp.bfloat16
    )
    hidden, gate_grad, up_grad, inputs, route_grad, returned = run_window(
        token_rows, scaled_rows, w_gate, w_up, w_down
    )
    grad_w_gate = contract_rows(inputs, gate_grad).astype(jnp.bfloat16)
    grad_w_up = contract_rows(inputs, up_grad).astype(jnp.bfloat16)
    grad_w_down = contract_rows(hidden, route_grad).astype(jnp.bfloat16)
    sums = jnp.sum(
        returned.astype(jnp.float32).reshape(2, EXPERTS, members, capacity, features), axis=2
    ).reshape(2, EXPERTS * capacity, features)
    mixed = jnp.dot(jnp.transpose(weighted), sums[0], precision=highest).astype(jnp.bfloat16)
    token_grad = jnp.dot(jnp.transpose(select), sums[1], precision=highest).astype(jnp.bfloat16)
    return (mixed, token_grad, grad_w_gate, grad_w_up, grad_w_down)


def solution(mesh):
    placed = (
        P("dp", "eshard"),
        P("dp", "eshard"),
        P("dp", None),
        P("dp", None),
        P("eshard", "dp"),
        P("eshard", "dp"),
        P("dp", "eshard"),
    )
    return jax.shard_map(
        on_device,
        mesh=mesh,
        in_specs=placed,
        out_specs=(
            P("dp", "eshard"),
            P("dp", "eshard"),
            P("eshard", "dp"),
            P("eshard", "dp"),
            P("dp", "eshard"),
        ),
        check_vma=False,
    )
```

time: 232 us -> 134 us (0.58)
  waiting for transfers between devices: 122 us -> 0 us
  Pallas kernels: 0 us -> 104 us
  matrix products: 59.9 us -> 25.3 us
  blocking collectives: 21.2 us -> 0 us
  between operations: 14.2 us -> 0.7 us
  starting transfers between devices: 7.69 us -> 0 us
    pallas_call x0 -> x1, Pallas kernels: none -> 104 us  [run_window(): pl.pallas_call(functools.partial(window_kernel, size, groups, members, ch...]
    reduce_scatter x3 -> x0, waiting for transfers between devices: 61.3 us -> none  [the longest x1 28.7 us: on_device(): lax.psum_scatter(up_part.astype(jnp.bfloat16), 'eshard', scatter_dimensio...]
    all_gather x3 -> x0, waiting for transfers between devices: 54.9 us -> none  [the longest x2 48.3 us: on_device(): lax.all_gather(for_sending(derivative(grad_hidden, gate_pre, up_pre)), 'e...]
    dot_general x8 -> x2, matrix products: 42 us -> 3.65 us  [the longest x1 1.83 us: on_device(): jnp.dot(jnp.transpose(select), sums[1], precision=highest)]
    all_to_all x2 -> x0, blocking collectives: 21.2 us -> none  [the longest x1 11.9 us: on_device(): lax.all_to_all(send_tokens, 'dp', split_axis=0, concat_axis=0, tiled=True)]
    all_to_all x2 -> x0, starting transfers between devices: 7.44 us -> none  [the longest x1 3.79 us: on_device(): lax.all_to_all(back_part.astype(jnp.bfloat16), 'dp', split_axis=0, concat...]
    all_to_all x2 -> x0, waiting for transfers between devices: 5.05 us -> none  [the longest x1 5.04 us: on_device(): lax.all_to_all(out_part.astype(jnp.bfloat16), 'dp', split_axis=0, concat_...]
  transfers between devices with their start and end apart: 8 -> 0, of which waited for: 7 -> 0; matrix products, arithmetic and copies ran while one was open for 23% -> 0% of each run, Pallas kernels for 0% -> 0%
where the time goes in v1:
time: 134 us
  Pallas kernels  104 us (78%)
  matrix products  25.3 us (19%)
  other arithmetic  3.69 us (3%)
    pallas_call x1, Pallas kernels, run_window(): pl.pallas_call(functools.partial(window_kernel, size, groups, members, ch...  104 us
    dot_general x3, matrix products, contract_rows(): lax.dot_general(left, right, (((0,), (0,)), ((), ())), preferred_element_...  18.7 us

profile of v1, /device:TPU:0, one launch (start us, length us, event | category | flops | bytes accessed | tf_op | source)
XLA Modules:
  0.0 134.0 jit_solution(13306276540208646823)
XLA Ops:
  0.6 0.0 copy-start
  0.6 0.8 convert_reduce_fusion.1
  1.4 1.2 reduce-window.6
  2.6 0.1 slice.18
  2.7 0.1 copy.18
  2.9 0.1 copy.19
  2.9 0.1 add_bitcast_fusion
  3.0 0.1 fusion.5
  3.1 0.7 convert_multiply_fusion
  3.8 0.7 fusion.3
  4.5 0.0 copy-done
  4.5 1.0 convolution_convert_fusion.5.grd_ref
  5.6 1.9 %convolution_convert_fusion.6.tok_ref = bf16[64,1024]{1,0:T(8,128)(2,1)} fusion(bf16[256,1024]{1,0:T(8,128)(2,1)} %param.7, f32[64,256]{1,0:T(8,128)S(1)} %get-tuple-element.17), kind=kOutput, calls=%fused_computation.6 | convolution fusion | flops 33636352 | bytes 720896 | tf_op jit(solution)/shard_map/dot_general | solution.py:319
  7.5 104.0 %shard_map.110 = (bf16[128,4096]{1,0:T(8,128)(2,1)}, bf16[128,4096]{1,0:T(8,128)(2,1)}, bf16[128,4096]{1,0:T(8,128)(2,1)}, bf16[128,1024]{1,0:T(8,128)(2,1)}, bf...) custom-call(bf16[64,1024]{1,0:T(8,128)(2,1)} %convolution_convert_fusion.6.tok_ref, ...), custom_call_target="tpu_custom_call" | custom-call | tf_op jit(solution)/shard_map/pallas_call | solution.py:282
  111.5 0.0 copy-start.1
  111.5 0.0 copy-start.3
  111.5 7.1 %convolution_convert_fusion = bf16[4096,1024]{1,0:T(8,128)(2,1)} fusion(bf16[128,4096]{1,0:T(8,128)(2,1)} %get-tuple-element.15, bf16[128,1024]{1,0:T(8,128)(2,1)} %get-tuple-element.16), kind=kOutput, calls=%fused_computation | convolution fusion | flops 1077936128 | bytes 9699328 | tf_op jit(solution)/shard_map/dot_general | solution.py:43
  118.6 0.0 copy-start.2
  118.6 0.0 copy-done.1
  118.6 0.0 copy-done.3
  118.6 5.8 %convolution_convert_fusion.1 = bf16[1024,4096]{1,0:T(8,128)(2,1)} fusion(bf16[128,1024]{1,0:T(8,128)(2,1)S(1)} %copy-done.1, bf16[128,4096]{1,0:T(8,128)(2,1)S(1)} %copy-done.3), kind=kOutput, calls=%fused_computation.1 | convolution fusion | flops 1077936128 | bytes 9699328 | tf_op jit(solution)/shard_map/dot_general | solution.py:43
  124.4 0.0 copy-start.4
  124.4 0.0 copy-done.2
  124.4 5.8 %convolution_convert_fusion.2 = bf16[1024,4096]{1,0:T(8,128)(2,1)} fusion(bf16[128,1024]{1,0:T(8,128)(2,1)S(1)} %copy-done.1, bf16[128,4096]{1,0:T(8,128)(2,1)S(1)} %copy-done.2), kind=kOutput, calls=%fused_computation.2 | convolution fusion | flops 1077936128 | bytes 9699328 | tf_op jit(solution)/shard_map/dot_general | solution.py:43
  130.2 0.0 copy-done.4
  130.2 0.1 convert_reduce_fusion
  130.3 1.8 %convolution_convert_fusion.3 = bf16[256,1024]{1,0:T(8,128)(2,1)} fusion(f32[64,256]{1,0:T(8,128)S(1)} %get-tuple-element.17, f32[64,1024]{1,0:T(8,128)S(1)} %bitcast.34), kind=kOutput, calls=%fused_computation.3 | convolution fusion | flops 201588736 | bytes 851968 | tf_op jit(solution)/shard_map/dot_general | solution.py:335
  132.2 1.8 %convolution_convert_fusion.4 = bf16[256,1024]{1,0:T(8,128)(2,1)} fusion(f32[64,256]{1,0:T(8,128)S(1)} %get-tuple-element.18, f32[64,1024]{1,0:T(8,128)S(1)} %bitcast.33), kind=kOutput, calls=%fused_computation.4 | convolution fusion | flops 201588736 | bytes 851968 | tf_op jit(solution)/shard_map/dot_general | solution.py:334
  (6 shorter events, 0.2 us)
Async XLA Ops:
  0.6 3.9 %copy-start = (bf16[256,1024]{1,0:T(8,128)(2,1)S(1)}, bf16[256,1024]{1,0:T(8,128)(2,1)}, u32[]{:S(2)}) copy-start(bf16[256,1024]{1,0:T(8,128)(2,1)} %param.8) | copy-start | bytes 1572868
  111.5 7.2 %copy-start.1 = (bf16[128,1024]{1,0:T(8,128)(2,1)S(1)}, bf16[128,1024]{1,0:T(8,128)(2,1)}, u32[]{:S(2)}) copy-start(bf16[128,1024]{1,0:T(8,128)(2,1)} %get-tuple-element.12) | copy-start | bytes 786436
  111.5 7.1 %copy-start.3 = (bf16[128,4096]{1,0:T(8,128)(2,1)S(1)}, bf16[128,4096]{1,0:T(8,128)(2,1)}, u32[]{:S(2)}) copy-start(bf16[128,4096]{1,0:T(8,128)(2,1)} %get-tuple-element.14) | copy-start | bytes 3145732
  118.6 5.8 %copy-start.2 = (bf16[128,4096]{1,0:T(8,128)(2,1)S(1)}, bf16[128,4096]{1,0:T(8,128)(2,1)}, u32[]{:S(2)}) copy-start(bf16[128,4096]{1,0:T(8,128)(2,1)} %get-tuple-element.13) | copy-start | bytes 3145732
  124.4 5.8 %copy-start.4 = (bf16[2,8,16,1024]{3,2,1,0:T(8,128)(2,1)S(1)}, bf16[2,8,16,1024]{3,2,1,0:T(8,128)(2,1)}, u32[]{:S(2)}) copy-start(bf16[2,8,16,1024]{3,2,1,0:T(8,128)(2,1)} %get-tuple-element.11) | copy-start | bytes 1572868

commit v2 on v1

--- a/solution.py
+++ b/solution.py
@@ -13,23 +13,6 @@
 VMEM_BYTES = 60 * 1024 * 1024
 
 
-def routing(ids, gates):
-    expert_ids = jnp.arange(EXPERTS, dtype=jnp.int32)
-    hits = (ids[:, :, None] == expert_ids[None, None, :]).astype(jnp.int32)
-    hit_tok = jnp.sum(hits, axis=1)
-    gate_values = gates.astype(jnp.float32) / 65536.0
-    weight_tok = jnp.sum(hits.astype(jnp.float32) * gate_values[:, :, None], axis=1)
-    slots = jnp.cumsum(hit_tok, axis=0) - hit_tok
-    target = expert_ids[None, :] * CAP + slots
-    rows = jnp.arange(EXPERTS * CAP, dtype=jnp.int32)
-    match = (target[None, :, :] == rows[:, None, None]).astype(jnp.float32) * hit_tok[
-        None, :, :
-    ].astype(jnp.float32)
-    select = jnp.sum(match, axis=2)
-    weighted = jnp.sum(match * weight_tok[None, :, :], axis=2)
-    return (select, weighted)
-
-
 MESH = pl.DeviceIdType.MESH
 
 
@@ -39,21 +22,43 @@
     )
 
 
-def contract_rows(left, right):
-    return lax.dot_general(
-        left, right, (((0,), (0,)), ((), ())), preferred_element_type=jnp.float32
-    )
+def halves(value):
+    high = value.astype(jnp.bfloat16)
+    return high, (value - high.astype(jnp.float32)).astype(jnp.bfloat16)
+
+
+def routing(ids, gates, cap):
+    tokens = ids.shape[1]
+    f32 = jnp.float32
+    values = gates.astype(f32) * (1.0 / 65536.0)
+    hits, weights = [], []
+    for expert in range(EXPERTS):
+        named = (ids == expert).astype(f32)
+        hits.append(jnp.sum(named, axis=0, keepdims=True))
+        weights.append(jnp.sum(named * values, axis=0, keepdims=True))
+    hit = jnp.concatenate(hits, axis=0)
+    earlier = (
+        lax.broadcasted_iota(jnp.int32, (tokens, tokens), 0)
+        < lax.broadcasted_iota(jnp.int32, (tokens, tokens), 1)
+    ).astype(jnp.bfloat16)
+    slots = jnp.dot(hit.astype(jnp.bfloat16), earlier, preferred_element_type=f32)
+    places = lax.broadcasted_iota(jnp.int32, (cap, tokens), 0).astype(f32)
+    select, weighted = [], []
+    for expert in range(EXPERTS):
+        here = (places == slots[expert : expert + 1]).astype(f32) * hits[expert]
+        select.append(here)
+        weighted.append(here * weights[expert])
+    return jnp.concatenate(select, axis=0), jnp.concatenate(weighted, axis=0)
 
 
 def window_kernel(
     size, groups, members, chunks, width,
-    tok_ref, grd_ref, wg_ref, wu_ref, wd_ref,
-    hid_ref, gg_ref, ug_ref, x_ref, g_ref, back_ref,
-    wg_v, wu_v, wd_v, x_v, g_v, part, outer, inner, full, out_acc, back_acc, y_send, y_recv,
+    cap, ids_ref, gates_ref, tokens_ref, cot_ref, wg_ref, wu_ref, wd_ref,
+    hid_ref, gg_ref, ug_ref, xt_ref, g_ref, back_ref, pick_ref,
+    tok_ref, grd_ref, x_ref, wg_v, wu_v, wd_v, x_v, g_v, part, outer, inner, full, out_acc, back_acc, y_send, y_recv,
     w_sem, xs_sem, xr_sem, in_sem, outer_sem, inner_sem, out_sem, ys_sem, yr_sem,
 ):
     me, z = lax.axis_index("dp"), lax.axis_index("eshard")
-    cap = tok_ref.shape[0] // EXPERTS
     feats = tok_ref.shape[1]
     rows = groups * cap
     half = size // 2
@@ -91,6 +96,11 @@
     def _():
         pl.semaphore_signal(barrier, inc=1, device_id={"eshard": outward}, device_id_type=MESH)
 
+    select, weighted = routing(ids_ref[...], gates_ref[...], cap)
+    tok_ref[...] = jnp.dot(
+        select.astype(jnp.bfloat16), tokens_ref[...], preferred_element_type=jnp.float32
+    ).astype(jnp.bfloat16)
+
     pl.semaphore_wait(barrier, groups + jnp.where(tip, 0, 1))
 
     def row_copy(src, dst, which, k):
@@ -105,8 +115,7 @@
             device_id_type=MESH,
         )
 
-    for which, (src, dst) in enumerate(((tok_ref, x_v), (grd_ref, g_v))):
-
+    def send_rows(which, src, dst):
         @pl.loop(1, groups)
         def _(k):
             row_copy(src, dst, which, k).start()
@@ -114,16 +123,27 @@
         own = pl.multiple_of((me // members) * cap, cap)
         dst[me] = src[pl.ds(own, cap), :]
 
-    for which, (src, dst) in enumerate(((tok_ref, x_v), (grd_ref, g_v))):
-
+    def take_rows(which, src, dst):
         @pl.loop(1, groups)
         def _(k):
             row_copy(src, dst, which, k).wait()
 
-    x_ref[...] = x_v[...].reshape(rows, feats)
-    g_ref[...] = g_v[...].reshape(rows, feats)
+    send_rows(0, tok_ref, x_v)
+    high, low = halves(weighted)
+    grd_ref[...] = (
+        jnp.dot(high, cot_ref[...], preferred_element_type=jnp.float32)
+        + jnp.dot(low, cot_ref[...], preferred_element_type=jnp.float32)
+    ).astype(jnp.bfloat16)
+    send_rows(1, grd_ref, g_v)
+    pick_ref[0] = jnp.transpose(select).astype(jnp.bfloat16)
+    high, low = halves(jnp.transpose(weighted))
+    pick_ref[1] = high
+    pick_ref[2] = low
     out_acc[...] = jnp.zeros_like(out_acc)
     back_acc[...] = jnp.zeros_like(back_acc)
+
+    take_rows(0, tok_ref, x_v)
+    x_ref[...] = x_v[...].reshape(rows, feats)
 
     def to_outer(c, k):
         return pltpu.make_async_remote_copy(
@@ -162,6 +182,12 @@
             elif k == 1:
                 own = jnp.dot(x_ref[...], wu_v[c], preferred_element_type=jnp.float32)
             else:
+
+                @pl.when(c == 0)
+                def _():
+                    take_rows(1, grd_ref, g_v)
+                    g_ref[...] = g_v[...].reshape(rows, feats)
+
                 own = contract_cols(g_ref[...], wd_v[c])
 
             @pl.when(tip)
@@ -206,11 +232,12 @@
         gate, up, down = summed(0), summed(1), summed(2)
         logistic = 1.0 / (1.0 + jnp.exp(-gate))
         silu = gate * logistic
-        hidden = (silu * up).astype(jnp.bfloat16)
+        product = silu * up
+        hidden = product.astype(jnp.bfloat16)
         gate_grad = (down * up * logistic * (1.0 + gate * (1.0 - logistic))).astype(jnp.bfloat16)
         up_grad = (down * silu).astype(jnp.bfloat16)
         cols = pl.ds(pl.multiple_of(c * width, width), width)
-        hid_ref[:, cols] = hidden
+        hid_ref[cols, :] = jnp.transpose(product).astype(jnp.bfloat16)
         gg_ref[:, cols] = gate_grad
         ug_ref[:, cols] = up_grad
         out_acc[...] += jnp.dot(hidden, wd_v[c], preferred_element_type=jnp.float32)
@@ -228,6 +255,10 @@
         def _():
             finish(t - lag)
 
+        @pl.when(t == 1)
+        def _():
+            xt_ref[...] = jnp.transpose(x_ref[...].astype(jnp.float32)).astype(jnp.bfloat16)
+
     y_send[0] = out_acc[...].astype(jnp.bfloat16).reshape(groups, cap, feats)
     y_send[1] = back_acc[...].astype(jnp.bfloat16).reshape(groups, cap, feats)
 
@@ -265,11 +296,11 @@
     back_ref[...] = y_recv[...]
 
 
-def run_window(token_rows, scaled_rows, w_gate, w_up, w_down):
+def run_window(ids, gates, tokens, cotangent, w_gate, w_up, w_down):
     groups, size = lax.axis_size("dp"), lax.axis_size("eshard")
     members = groups // EXPERTS
     feats, hidden = w_gate.shape
-    cap = token_rows.shape[0] // EXPERTS
+    cap, count = CAP, tokens.shape[0]
     rows = groups * cap
     width = min(WIDTH, hidden)
     chunks = hidden // width
@@ -277,17 +308,22 @@
     vmem, hbm = pl.BlockSpec(memory_space=pltpu.VMEM), pl.BlockSpec(memory_space=pl.ANY)
     dma = pltpu.SemaphoreType.DMA
     wide = jax.ShapeDtypeStruct((rows, hidden), bf16)
-    deep = jax.ShapeDtypeStruct((rows, feats), bf16)
     stage = pltpu.VMEM((chunks, 3, rows, width), bf16)
     return pl.pallas_call(
-        functools.partial(window_kernel, size, groups, members, chunks, width),
+        functools.partial(window_kernel, size, groups, members, chunks, width, cap),
         out_shape=(
-            wide, wide, wide, deep, deep,
+            jax.ShapeDtypeStruct((hidden, rows), bf16), wide, wide,
+            jax.ShapeDtypeStruct((feats, rows), bf16),
+            jax.ShapeDtypeStruct((rows, feats), bf16),
             jax.ShapeDtypeStruct((2, groups, cap, feats), bf16),
+            jax.ShapeDtypeStruct((3, count, EXPERTS * cap), bf16),
         ),
-        in_specs=[vmem, vmem, hbm, hbm, hbm],
-        out_specs=(vmem,) * 6,
+        in_specs=[vmem, vmem, vmem, vmem, hbm, hbm, hbm],
+        out_specs=(vmem,) * 7,
         scratch_shapes=[
+            pltpu.VMEM((EXPERTS * cap, feats), bf16),
+            pltpu.VMEM((EXPERTS * cap, feats), bf16),
+            pltpu.VMEM((rows, feats), bf16),
             pltpu.VMEM((chunks, feats, width), bf16),
             pltpu.VMEM((chunks, feats, width), bf16),
             pltpu.VMEM((chunks, width, feats), bf16),
@@ -306,34 +342,85 @@
         compiler_params=pltpu.CompilerParams(
             collective_id=0, has_side_effects=True, vmem_limit_bytes=VMEM_BYTES
         ),
-    )(token_rows, scaled_rows, w_gate, w_up, w_down)
+    )(ids, gates, tokens, cotangent, w_gate, w_up, w_down)
+
+
+def gradient_kernel(
+    members, xt_ref, gg_ref, ug_ref, hid_ref, g_ref, back_ref, pick_ref,
+    mixed_ref, token_ref, gate_ref, up_ref, down_ref,
+):
+    f32, bf16 = jnp.float32, jnp.bfloat16
+
+    def product(left, right):
+        return jnp.dot(left, right, preferred_element_type=f32)
+
+    gate_ref[...] = product(xt_ref[...], gg_ref[...]).astype(bf16)
+    up_ref[...] = product(xt_ref[...], ug_ref[...]).astype(bf16)
+    down_ref[...] = product(hid_ref[...], g_ref[...]).astype(bf16)
+
+    @pl.when(pl.program_id(0) == 0)
+    def _():
+        def gathered(which):
+            parts = []
+            for expert in range(EXPERTS):
+                total = back_ref[which, expert * members].astype(f32)
+                for member in range(1, members):
+                    total = total + back_ref[which, expert * members + member].astype(f32)
+                parts.append(total)
+            return halves(jnp.concatenate(parts, axis=0))
+
+        high, low = gathered(0)
+        mixed_ref[...] = (
+            product(pick_ref[1], high) + product(pick_ref[2], high) + product(pick_ref[1], low)
+        ).astype(bf16)
+        high, low = gathered(1)
+        token_ref[...] = (product(pick_ref[0], high) + product(pick_ref[0], low)).astype(bf16)
+
+
+def run_gradients(count, hidden_t, gate_grad, up_grad, inputs_t, route_grad, back, pick):
+    groups = lax.axis_size("dp")
+    feats, rows = inputs_t.shape
+    hidden = hidden_t.shape[0]
+    cap = back.shape[2]
+    width = min(2 * WIDTH, hidden)
+    bf16 = jnp.bfloat16
+
+    def whole(shape):
+        return pl.BlockSpec(shape, lambda i: (0,) * len(shape))
+
+    across = pl.BlockSpec((rows, width), lambda i: (0, i))
+    return pl.pallas_call(
+        functools.partial(gradient_kernel, groups // EXPERTS),
+        grid=(hidden // width,),
+        out_shape=(
+            jax.ShapeDtypeStruct((count, feats), bf16),
+            jax.ShapeDtypeStruct((count, feats), bf16),
+            jax.ShapeDtypeStruct((feats, hidden), bf16),
+            jax.ShapeDtypeStruct((feats, hidden), bf16),
+            jax.ShapeDtypeStruct((hidden, feats), bf16),
+        ),
+        in_specs=[
+            whole((feats, rows)), across, across,
+            pl.BlockSpec((width, rows), lambda i: (i, 0)),
+            whole((rows, feats)), whole((2, groups, cap, feats)), whole(pick.shape),
+        ],
+        out_specs=(
+            whole((count, feats)), whole((count, feats)),
+            pl.BlockSpec((feats, width), lambda i: (0, i)),
+            pl.BlockSpec((feats, width), lambda i: (0, i)),
+            pl.BlockSpec((width, feats), lambda i: (i, 0)),
+        ),
+        compiler_params=pltpu.CompilerParams(vmem_limit_bytes=VMEM_BYTES),
+    )(inputs_t, gate_grad, up_grad, hidden_t, route_grad, back, pick)
 
 
 def on_device(tokens, cotangent, route_ids, gate_fixed, w_gate, w_up, w_down):
-    groups = lax.axis_size("dp")
-    members = groups // EXPERTS
-    features = tokens.shape[1]
-    highest = lax.Precision.HIGHEST
-    select, weighted = routing(route_ids, gate_fixed)
-    capacity = select.shape[0] // EXPERTS
-    token_rows = jnp.dot(
-        select.astype(jnp.bfloat16), tokens, preferred_element_type=jnp.float32
-    ).astype(jnp.bfloat16)
-    scaled_rows = jnp.dot(weighted, cotangent.astype(jnp.float32), precision=highest).astype(
-        jnp.bfloat16
+    hidden_t, gate_grad, up_grad, inputs_t, route_grad, back, pick = run_window(
+        jnp.transpose(route_ids), jnp.transpose(gate_fixed), tokens, cotangent, w_gate, w_up, w_down
     )
-    hidden, gate_grad, up_grad, inputs, route_grad, returned = run_window(
-        token_rows, scaled_rows, w_gate, w_up, w_down
+    return run_gradients(
+        tokens.shape[0], hidden_t, gate_grad, up_grad, inputs_t, route_grad, back, pick
     )
-    grad_w_gate = contract_rows(inputs, gate_grad).astype(jnp.bfloat16)
-    grad_w_up = contract_rows(inputs, up_grad).astype(jnp.bfloat16)
-    grad_w_down = contract_rows(hidden, route_grad).astype(jnp.bfloat16)
-    sums = jnp.sum(
-        returned.astype(jnp.float32).reshape(2, EXPERTS, members, capacity, features), axis=2
-    ).reshape(2, EXPERTS * capacity, features)
-    mixed = jnp.dot(jnp.transpose(weighted), sums[0], precision=highest).astype(jnp.bfloat16)
-    token_grad = jnp.dot(jnp.transpose(select), sums[1], precision=highest).astype(jnp.bfloat16)
-    return (mixed, token_grad, grad_w_gate, grad_w_up, grad_w_down)
 
 
 def solution(mesh):

time: 134 us -> 119 us (0.89)
  matrix products: 25.3 us -> 0 us
  Pallas kernels: 104 us -> 118 us
  other arithmetic: 3.69 us -> 0 us
    dot_general x7 -> x0, matrix products: 25.3 us -> none  [the longest x3 18.7 us: contract_rows(): lax.dot_general(left, right, (((0,), (0,)), ((), ())), preferred_element_...]
    pallas_call x0 -> x1, Pallas kernels: none -> 14.5 us  [run_gradients(): pl.pallas_call(functools.partial(gradient_kernel, groups // EXPERTS), gri...]
    reduce_sum x4 -> x0, other arithmetic: 1.6 us -> none  [the longest x1 0.75 us: routing(): hit_tok = jnp.sum(hits, axis=1)]
where the time goes in v2:
time: 119 us; the launch traced here: 118 us
  Pallas kernels  118 us (99%)
    pallas_call x1, Pallas kernels, run_window(): pl.pallas_call(functools.partial(window_kernel, size, groups, members, ch...  103 us
    pallas_call x1, Pallas kernels, run_gradients(): pl.pallas_call(functools.partial(gradient_kernel, groups // EXPERTS), gri...  14.5 us

profile of v2, /device:TPU:0, one launch (start us, length us, event | category | flops | bytes accessed | tf_op | source)
XLA Modules:
  0.0 118.4 jit_solution(586367092274774623)
XLA Ops:
  0.6 103.2 %shard_map.110 = (bf16[4096,128]{1,0:T(8,128)(2,1)}, bf16[128,4096]{1,0:T(8,128)(2,1)}, bf16[128,4096]{1,0:T(8,128)(2,1)}, bf16[1024,128]{1,0:T(8,128)(2,1)}, bf...) custom-call(s32[2,256]{1,0:T(2,128)} %bitcast.2, s32[2,256]{1,0:T(2,128)} %bitcast.3, ...), custom_call_target="tpu_custom_call" | custom-call | tf_op jit(solution)/shard_map/pallas_call | solution.py:312
  103.9 14.5 %shard_map.111 = (bf16[256,1024]{1,0:T(8,128)(2,1)}, bf16[256,1024]{1,0:T(8,128)(2,1)}, bf16[1024,4096]{1,0:T(8,128)(2,1)}, bf16[1024,4096]{1,0:T(8,128)(2,1)}, bf16[4096,1024]{1,0:T(8,128)(2,1)}) custom-call(bf16[1024,128]{1,0:T(8,128)(2,1)} %get-tuple-element.12.xt_ref, bf16[128,4096]{1,0:T(8,128)(2,1)} %get-tuple-element.13.gg_ref, ...), custom_call_target="tpu_custom_call" | custom-call | tf_op jit(solution)/shard_map/pallas_call | solution.py:392

commit v3 on v2

--- a/solution.py
+++ b/solution.py
@@ -10,7 +10,8 @@
 EXPERTS = 4
 CAP = 16
 WIDTH = 256
-VMEM_BYTES = 60 * 1024 * 1024
+VMEM_BYTES = 46 * 1024 * 1024
+GRAD_BYTES = 24 * 1024 * 1024
 
 
 MESH = pl.DeviceIdType.MESH
@@ -173,6 +174,16 @@
             device_id={"eshard": outward}, device_id_type=MESH,
         )
 
+    def forward(c, k):
+        to_partner(c, k).wait_recv()
+        full[c, k] = (
+            part[c, k].astype(jnp.float32) + inner[c, k].astype(jnp.float32)
+        ).astype(jnp.bfloat16)
+
+        @pl.when(jnp.logical_not(tip))
+        def _():
+            sum_out(c, k).start()
+
     def gather_in(c):
         for copy in weight_copies(c):
             copy.wait()
@@ -207,41 +218,68 @@
             def _():
                 to_outer(c, k).start()
 
+            @pl.when(jnp.logical_and(middle, c > 0))
+            def _():
+                forward(c - 1, k)
+
+    def return_copy(which, k):
+        to = lax.rem(me + k, groups)
+        return pltpu.make_async_remote_copy(
+            src_ref=y_send.at[which, to], dst_ref=y_recv.at[which, me],
+            send_sem=ys_sem.at[which, k], recv_sem=yr_sem.at[which, k],
+            device_id={"dp": to}, device_id_type=MESH,
+        )
+
+    def send_home(which, total):
+        y_send[which] = total[...].astype(jnp.bfloat16).reshape(groups, cap, feats)
+
+        @pl.loop(1, groups)
+        def _(k):
+            return_copy(which, k).start()
+
+        y_recv[which, me] = y_send[which, me]
+
     def finish(c):
-        for k in range(3):
-            to_partner(c, k).wait_recv()
-
-            @pl.when(middle)
-            def _():
-                full[c, k] = (
-                    part[c, k].astype(jnp.float32) + inner[c, k].astype(jnp.float32)
-                ).astype(jnp.bfloat16)
-
-            @pl.when(jnp.logical_and(middle, jnp.logical_not(tip)))
-            def _():
-                sum_out(c, k).start()
+        def summed(k):
+            @pl.when(jnp.logical_not(middle))
+            def _():
+                to_partner(c, k).wait_recv()
 
             @pl.when(jnp.logical_not(jnp.logical_or(middle, tip)))
             def _():
                 pass_out(c, k).start()
 
-        def summed(k):
+            @pl.when(jnp.logical_and(middle, c == chunks - 1))
+            def _():
+                forward(c, k)
+
             mine = part[c, k].astype(jnp.float32)
             return inner[c, k].astype(jnp.float32) + jnp.where(middle, mine, jnp.zeros_like(mine))
 
-        gate, up, down = summed(0), summed(1), summed(2)
+        gate, up = summed(0), summed(1)
         logistic = 1.0 / (1.0 + jnp.exp(-gate))
         silu = gate * logistic
         product = silu * up
         hidden = product.astype(jnp.bfloat16)
+        cols = pl.ds(pl.multiple_of(c * width, width), width)
+        out_acc[...] += jnp.dot(hidden, wd_v[c], preferred_element_type=jnp.float32)
+
+        @pl.when(c == chunks - 1)
+        def _():
+            send_home(0, out_acc)
+
+        down = summed(2)
         gate_grad = (down * up * logistic * (1.0 + gate * (1.0 - logistic))).astype(jnp.bfloat16)
         up_grad = (down * silu).astype(jnp.bfloat16)
-        cols = pl.ds(pl.multiple_of(c * width, width), width)
-        hid_ref[cols, :] = jnp.transpose(product).astype(jnp.bfloat16)
+        back_acc[...] += contract_cols(gate_grad, wg_v[c]) + contract_cols(up_grad, wu_v[c])
+
+        @pl.when(c == chunks - 1)
+        def _():
+            send_home(1, back_acc)
+
         gg_ref[:, cols] = gate_grad
         ug_ref[:, cols] = up_grad
-        out_acc[...] += jnp.dot(hidden, wd_v[c], preferred_element_type=jnp.float32)
-        back_acc[...] += contract_cols(gate_grad, wg_v[c]) + contract_cols(up_grad, wu_v[c])
+        hid_ref[cols, :] = jnp.transpose(product).astype(jnp.bfloat16)
 
     lag = jnp.where(middle, 1, 1 + 4 * distance)
 
@@ -258,25 +296,6 @@
         @pl.when(t == 1)
         def _():
             xt_ref[...] = jnp.transpose(x_ref[...].astype(jnp.float32)).astype(jnp.bfloat16)
-
-    y_send[0] = out_acc[...].astype(jnp.bfloat16).reshape(groups, cap, feats)
-    y_send[1] = back_acc[...].astype(jnp.bfloat16).reshape(groups, cap, feats)
-
-    def return_copy(which, k):
-        to = lax.rem(me + k, groups)
-        return pltpu.make_async_remote_copy(
-            src_ref=y_send.at[which, to], dst_ref=y_recv.at[which, me],
-            send_sem=ys_sem.at[which, k], recv_sem=yr_sem.at[which, k],
-            device_id={"dp": to}, device_id_type=MESH,
-        )
-
-    for which in range(2):
-
-        @pl.loop(1, groups)
-        def _(k):
-            return_copy(which, k).start()
-
-        y_recv[which, me] = y_send[which, me]
 
     @pl.loop(0, chunks)
     def _(c):
@@ -382,7 +401,7 @@
     feats, rows = inputs_t.shape
     hidden = hidden_t.shape[0]
     cap = back.shape[2]
-    width = min(2 * WIDTH, hidden)
+    width = min(4 * WIDTH, hidden)
     bf16 = jnp.bfloat16
 
     def whole(shape):
@@ -410,7 +429,7 @@
             pl.BlockSpec((feats, width), lambda i: (0, i)),
             pl.BlockSpec((width, feats), lambda i: (i, 0)),
         ),
-        compiler_params=pltpu.CompilerParams(vmem_limit_bytes=VMEM_BYTES),
+        compiler_params=pltpu.CompilerParams(vmem_limit_bytes=GRAD_BYTES),
     )(inputs_t, gate_grad, up_grad, hidden_t, route_grad, back, pick)
 
 

time: 119 us -> 113 us (0.950)
  Pallas kernels: 118 us -> 108 us
  local copies, waits for them, and re-layouts: 0 us -> 3.44 us
    pallas_call x1, Pallas kernels: 103 us -> 96.2 us  [run_window(): pl.pallas_call(functools.partial(window_kernel, size, groups, members, ch...]
    unnamed x0 -> x8, local copies, waits for them, and re-layouts: none -> 3.44 us
    pallas_call x1, Pallas kernels: 14.5 us -> 12.1 us  [run_gradients(): pl.pallas_call(functools.partial(gradient_kernel, groups // EXPERTS), gri...]
where the time goes in v3:
time: 113 us; the launch traced here: 112 us
  Pallas kernels  108 us (96%)
  local copies, waits for them, and re-layouts  3.44 us (3%)
    pallas_call x1, Pallas kernels, run_window(): pl.pallas_call(functools.partial(window_kernel, size, groups, members, ch...  96.2 us
    pallas_call x1, Pallas kernels, run_gradients(): pl.pallas_call(functools.partial(gradient_kernel, groups // EXPERTS), gri...  12.1 us
    unnamed x8, local copies, waits for them, and re-layouts  3.44 us

profile of v3, /device:TPU:0, one launch (start us, length us, event | category | flops | bytes accessed | tf_op | source)
XLA Modules:
  0.0 112.4 jit_solution(17150980349333036936)
XLA Ops:
  0.6 0.0 copy-start
  0.6 1.0 copy-done
  1.7 0.0 copy-start.1
  1.7 1.0 copy-done.1
  2.7 0.0 copy-start.2
  2.7 0.7 copy-done.2
  3.4 0.0 copy-start.3
  3.4 0.7 copy-done.3
  4.1 96.2 %shard_map.110 = (bf16[4096,128]{1,0:T(8,128)(2,1)S(1)}, bf16[128,4096]{1,0:T(8,128)(2,1)S(1)}, bf16[128,4096]{1,0:T(8,128)(2,1)S(1)}, bf16[1024,128]{1,0:T(8,12...) custom-call(s32[2,256]{1,0:T(2,128)S(1)} %bitcast.2, ...), custom_call_target="tpu_custom_call" | custom-call | tf_op jit(solution)/shard_map/pallas_call | solution.py:331
  100.3 12.1 %shard_map.111 = (bf16[256,1024]{1,0:T(8,128)(2,1)}, bf16[256,1024]{1,0:T(8,128)(2,1)}, bf16[1024,4096]{1,0:T(8,128)(2,1)}, bf16[1024,4096]{1,0:T(8,128)(2,1)}, bf16[4096,1024]{1,0:T(8,128)(2,1)}) custom-call(bf16[1024,128]{1,0:T(8,128)(2,1)S(1)} %get-tuple-element.12.xt_ref, bf16[128,4096]{1,0:T(8,128)(2,1)S(1)} %get-tuple-element.13.gg_ref, ...), custom_call_target="tpu_custom_call" | custom-call | tf_op jit(solution)/shard_map/pallas_call | solution.py:411
Async XLA Ops:
  0.6 1.0 copy-start
  1.7 1.0 copy-start.1
  2.7 0.7 copy-start.2
  3.4 0.7 copy-start.3
